TPU v7x, 32 devices: a whole 2x2x4 slice. The times are simulated.
32 devices in a mesh: pipe: 4 (over x, core), dp: 2 (over y), tensor: 4 (over z).
Axes of the slice: x: 2, y: 2, z: 4, core: 2. Of those that a mesh axis runs over, the one named last changes fastest.
Arguments:
- grad_top: bfloat16 [2, 128, 12288], P(None, None, ('dp', 'tensor')), may hold values from -1.1953125 to 1.1953125
- inputs: bfloat16 [4, 2, 128, 12288], P('pipe', None, None, ('dp', 'tensor')), may hold values from -6 to 6
- pre: bfloat16 [4, 2, 128, 6144], P('pipe', None, 'dp', 'tensor'), may hold values from -6 to 6
- weight_in: bfloat16 [4, 6144, 12288], P('pipe', 'tensor', 'dp'), may hold values from -0.0546875 to 0.0546875
- weight_out: bfloat16 [4, 6144, 12288], P('pipe', 'tensor', 'dp'), may hold values from -0.0546875 to 0.0546875
Outputs:
- weight_in_grad: bfloat16 [4, 6144, 12288], P('pipe', 'tensor', 'dp')
- weight_out_grad: bfloat16 [4, 6144, 12288], P('pipe', 'tensor', 'dp')
- section_grads: bfloat16 [4, 2, 128, 12288], P('pipe', None, None, ('dp', 'tensor'))
All inputs are finite; a program needn't handle non-finite values.
Results may differ from a plain program's by a relative error of at most 0.024.
Values may be sent and summed in bfloat16 or wider, within the bound.
A program may use at most 512 MiB of HBM per device.

v0:
```python
import math

import jax
import jax.numpy as jnp
from jax import lax
from jax.sharding import PartitionSpec as P


def shifted(block, axis, distance):
    devices = range(lax.axis_size(axis))
    route = [(i - distance, i) for i in devices if i - distance in devices]
    return lax.ppermute(block, axis, route)


def gelu_pair(values):
    root_coef = math.sqrt(2.0 / math.pi)
    inner = root_coef * (values + 0.044715 * values * values * values)
    tangent = jnp.tanh(inner)
    activ = 0.5 * values * (1.0 + tangent)
    slope = 0.5 * (1.0 + tangent) + 0.5 * values * (1.0 - tangent * tangent) * root_coef * (
        1.0 + 3.0 * 0.044715 * values * values
    )
    return (activ, slope)


def on_device(grad_top, inputs, pre, weight_in, weight_out):
    sections = lax.axis_size("pipe")
    section = lax.axis_index("pipe")
    micro = grad_top.shape[0]
    local_in = weight_in[0]
    local_out = weight_out[0]
    contract = (((0,), (0,)), ((), ()))
    accum_in = jnp.zeros(local_in.shape, jnp.float32)
    accum_out = jnp.zeros(local_out.shape, jnp.float32)
    grads_out = jnp.zeros(grad_top.shape, jnp.bfloat16)
    outgoing = grad_top[0]
    for timestep in range(micro + sections - 1):
        micro_index = timestep - (sections - 1 - section)
        valid = jnp.logical_and(micro_index >= 0, micro_index < micro)
        clipped = jnp.clip(micro_index, 0, micro - 1)
        top_grad = lax.dynamic_index_in_dim(grad_top, clipped, 0, False)
        if timestep == 0:
            current = top_grad
        else:
            received = shifted(outgoing, "pipe", -1)
            current = jnp.where(section == sections - 1, top_grad, received)
        layer_input = lax.dynamic_index_in_dim(inputs[0], clipped, 0, False)
        pre_local = lax.dynamic_index_in_dim(pre[0], clipped, 0, False)
        grad_cols, input_cols = (
            lax.all_gather(current, "tensor", axis=1, tiled=True),
            lax.all_gather(layer_input, "tensor", axis=1, tiled=True),
        )
        head_part = lax.dot_general(
            grad_cols, local_out, (((1,), (1,)), ((), ())), preferred_element_type=jnp.float32
        )
        head_grad = lax.psum(head_part.astype(jnp.bfloat16), "dp").astype(jnp.float32)
        pre_all = lax.all_gather(pre_local, "dp", axis=0, tiled=True)
        activ, slope = gelu_pair(pre_all.astype(jnp.float32))
        head_delta = (head_grad * slope).astype(jnp.bfloat16)
        activated = activ.astype(jnp.bfloat16)
        partial_value = jnp.dot(head_delta, local_in, preferred_element_type=jnp.float32)
        summed = lax.psum_scatter(
            partial_value.astype(jnp.bfloat16), "tensor", scatter_dimension=1, tiled=True
        ).astype(jnp.float32)
        new_grad = (current.astype(jnp.float32) + summed).astype(jnp.bfloat16)
        out_term = lax.dot_general(
            activated, grad_cols, contract, preferred_element_type=jnp.float32
        )
        in_term = lax.dot_general(
            head_delta, input_cols, contract, preferred_element_type=jnp.float32
        )
        accum_out = accum_out + jnp.where(valid, out_term, 0.0)
        accum_in = accum_in + jnp.where(valid, in_term, 0.0)
        previous = lax.dynamic_index_in_dim(grads_out, clipped, 0, False)
        grads_out = lax.dynamic_update_index_in_dim(
            grads_out, jnp.where(valid, new_grad, previous), clipped, 0
        )
        outgoing = new_grad
    return (
        accum_in.astype(jnp.bfloat16)[None],
        accum_out.astype(jnp.bfloat16)[None],
        grads_out[None],
    )


def solution(mesh):
    placed = (
        P(None, None, ("dp", "tensor")),
        P("pipe", None, None, ("dp", "tensor")),
        P("pipe", None, "dp", "tensor"),
        P("pipe", "tensor", "dp"),
        P("pipe", "tensor", "dp"),
    )
    return jax.shard_map(
        on_device,
        mesh=mesh,
        in_specs=placed,
        out_specs=(
            P("pipe", "tensor", "dp"),
            P("pipe", "tensor", "dp"),
            P("pipe", None, None, ("dp", "tensor")),
        ),
        check_vma=False,
    )
```

profile of v0, /device:TPU:0, one launch (start us, length us, event | category | flops | bytes accessed | tf_op | source)
XLA Modules:
  0.0 836.4 jit_solution(14600435980791823250)
XLA Ops:
  9.1 40.8 %all-gather.30.cloned.1.call-done = bf16[1,128,6144]{2,1,0:T(8,128)(2,1)} async-done(((bf16[1,128,1536]{2,1,0:T(8,128)(2,1)}), bf16[1,128,6144]{2,1,0:T(8,128)(2,1)}) %all-gather.30.cloned.1.call-update) | async-done | bytes 1572880 | tf_op jit(solution)/shard_map/all_gather | solution.py:50
  49.9 14.0 %fusion.37 = bf16[128,1536]{1,0:T(8,128)(2,1)} fusion(bf16[1,1536,6144]{2,1,0:T(8,128)(2,1)} %param.9, bf16[1,128,6144]{2,1,0:T(8,128)(2,1)} %all-gather.30.cloned.1.call-done), kind=kOutput, calls=%fused_computation.29 | convolution fusion | flops 2416115712 | bytes 20840448 | tf_op jit(solution)/shard_map/dot_general | solution.py:53
  64.8 9.4 %all-gather.1 = bf16[1,1,128,1536]{3,2,1,0:T(8,128)(2,1)S(1)} all-gather(bf16[1,1,64,1536]{3,2,1,0:T(8,128)(2,1)S(1)} %get-tuple-element.19), channel_id=3, replica_groups=mesh['pipe'=4,'dp'=2,'tensor'=4] {'dp'}, dimensions={2}, use_global_device_ids=true | all-gather | bytes 589824 | tf_op jit(solution)/shard_map/all_gather | solution.py:57
  74.2 15.2 %all-reduce.6.cloned.1.call-done = bf16[128,1536]{1,0:T(8,128)(2,1)} async-done(((bf16[128,1536]{1,0:T(8,128)(2,1)}), bf16[128,1536]{1,0:T(8,128)(2,1)}) %all-reduce.6.cloned.1.call-update) | async-done | bytes 393232 | tf_op jit(solution)/shard_map/psum | solution.py:56
  89.5 10.7 %fusion.22 = bf16[128,6144]{1,0:T(8,128)(2,1)} fusion(bf16[1,1536,6144]{2,1,0:T(8,128)(2,1)} %param.8, bf16[128,1536]{1,0:T(8,128)(2,1)} %all-reduce.6.cloned.1.call-done, bf16[1,1,128,1536]{3,2,1,0:T(8,128)(2,1)S(1)} %all-gather.1), kind=kOutput, calls=%fused_computation.24 | convolution fusion | flops 2420834304 | bytes 21233664 | tf_op jit(solution)/shard_map/dot_general | solution.py:61
  100.2 35.5 %reduce-scatter.6.cloned.1.call-done = bf16[128,1536]{1,0:T(8,128)(2,1)} async-done(((bf16[128,6144]{1,0:T(8,128)(2,1)}), bf16[128,1536]{1,0:T(8,128)(2,1)}) %reduce-scatter.6.cloned.1.call-update) | async-done | bytes 393232 | tf_op jit(solution)/shard_map/reduce_scatter | solution.py:62
  138.3 2.3 collective-permute-done
  141.7 39.8 %all-gather.22.cloned.1.call-done = bf16[128,6144]{1,0:T(8,128)(2,1)} async-done(((bf16[128,1536]{1,0:T(8,128)(2,1)}), bf16[128,6144]{1,0:T(8,128)(2,1)}) %all-gather.22.cloned.1.call-update) | async-done | bytes 1572880 | tf_op jit(solution)/shard_map/all_gather | solution.py:50
  181.5 14.0 %fusion.40 = bf16[128,1536]{1,0:T(8,128)(2,1)} fusion(bf16[128,6144]{1,0:T(8,128)(2,1)} %all-gather.22.cloned.1.call-done, bf16[1,1536,6144]{2,1,0:T(8,128)(2,1)} %param.9), kind=kOutput, calls=%fused_computation.30 | convolution fusion | flops 2416115712 | bytes 20840448 | tf_op jit(solution)/shard_map/dot_general | solution.py:53
  195.6 8.2 all-gather.3
  203.8 16.6 %all-reduce.8.cloned.1.call-done = bf16[128,1536]{1,0:T(8,128)(2,1)} async-done(((bf16[128,1536]{1,0:T(8,128)(2,1)}), bf16[128,1536]{1,0:T(8,128)(2,1)}) %all-reduce.8.cloned.1.call-update) | async-done | bytes 393232 | tf_op jit(solution)/shard_map/psum | solution.py:56
  220.4 10.7 %fusion.25 = bf16[128,6144]{1,0:T(8,128)(2,1)} fusion(bf16[1,1536,6144]{2,1,0:T(8,128)(2,1)} %param.8, bf16[128,1536]{1,0:T(8,128)(2,1)} %all-reduce.8.cloned.1.call-done, bf16[1,1,128,1536]{3,2,1,0:T(8,128)(2,1)S(1)} %all-gather.3), kind=kOutput, calls=%fused_computation.25 | convolution fusion | flops 2420834304 | bytes 21233664 | tf_op jit(solution)/shard_map/dot_general | solution.py:61
  231.2 35.5 %reduce-scatter.8.cloned.1.call-done = bf16[128,1536]{1,0:T(8,128)(2,1)} async-done(((bf16[128,6144]{1,0:T(8,128)(2,1)}), bf16[128,1536]{1,0:T(8,128)(2,1)}) %reduce-scatter.8.cloned.1.call-update) | async-done | bytes 393232 | tf_op jit(solution)/shard_map/reduce_scatter | solution.py:62
  269.2 2.3 collective-permute-done.1
  272.9 39.5 %all-gather.24.cloned.1.call-done = bf16[128,6144]{1,0:T(8,128)(2,1)} async-done(((bf16[128,1536]{1,0:T(8,128)(2,1)}), bf16[128,6144]{1,0:T(8,128)(2,1)}) %all-gather.24.cloned.1.call-update) | async-done | bytes 1572880 | tf_op jit(solution)/shard_map/all_gather | solution.py:50
  312.4 14.0 %fusion.43 = bf16[128,1536]{1,0:T(8,128)(2,1)} fusion(bf16[128,6144]{1,0:T(8,128)(2,1)} %all-gather.24.cloned.1.call-done, bf16[1,1536,6144]{2,1,0:T(8,128)(2,1)} %param.9), kind=kOutput, calls=%fused_computation.31 | convolution fusion | flops 2416115712 | bytes 20840448 | tf_op jit(solution)/shard_map/dot_general | solution.py:53
  326.5 8.3 all-gather.5
  334.7 16.6 %all-reduce.10.cloned.1.call-done = bf16[128,1536]{1,0:T(8,128)(2,1)} async-done(((bf16[128,1536]{1,0:T(8,128)(2,1)}), bf16[128,1536]{1,0:T(8,128)(2,1)}) %all-reduce.10.cloned.1.call-update) | async-done | bytes 393232 | tf_op jit(solution)/shard_map/psum | solution.py:56
  351.3 10.7 %fusion.28 = bf16[128,6144]{1,0:T(8,128)(2,1)} fusion(bf16[1,1536,6144]{2,1,0:T(8,128)(2,1)} %param.8, bf16[128,1536]{1,0:T(8,128)(2,1)} %all-reduce.10.cloned.1.call-done, bf16[1,1,128,1536]{3,2,1,0:T(8,128)(2,1)S(1)} %all-gather.5), kind=kOutput, calls=%fused_computation.26 | convolution fusion | flops 2420834304 | bytes 21233664 | tf_op jit(solution)/shard_map/dot_general | solution.py:61
  362.1 35.5 %reduce-scatter.10.cloned.1.call-done = bf16[128,1536]{1,0:T(8,128)(2,1)} async-done(((bf16[128,6144]{1,0:T(8,128)(2,1)}), bf16[128,1536]{1,0:T(8,128)(2,1)}) %reduce-scatter.10.cloned.1.call-update) | async-done | bytes 393232 | tf_op jit(solution)/shard_map/reduce_scatter | solution.py:62
  400.1 2.3 collective-permute-done.2
  403.4 39.9 %all-gather.26.cloned.1.call-done = bf16[128,6144]{1,0:T(8,128)(2,1)} async-done(((bf16[128,1536]{1,0:T(8,128)(2,1)}), bf16[128,6144]{1,0:T(8,128)(2,1)}) %all-gather.26.cloned.1.call-update) | async-done | bytes 1572880 | tf_op jit(solution)/shard_map/all_gather | solution.py:50
  443.3 14.0 %fusion.46 = bf16[128,1536]{1,0:T(8,128)(2,1)} fusion(bf16[128,6144]{1,0:T(8,128)(2,1)} %all-gather.26.cloned.1.call-done, bf16[1,1536,6144]{2,1,0:T(8,128)(2,1)} %param.9), kind=kOutput, calls=%fused_computation.32 | convolution fusion | flops 2416115712 | bytes 20840448 | tf_op jit(solution)/shard_map/dot_general | solution.py:53
  457.3 7.8 all-gather.7
  465.2 16.9 %all-reduce.12.cloned.1.call-done = bf16[128,1536]{1,0:T(8,128)(2,1)} async-done(((bf16[128,1536]{1,0:T(8,128)(2,1)}), bf16[128,1536]{1,0:T(8,128)(2,1)}) %all-reduce.12.cloned.1.call-update) | async-done | bytes 393232 | tf_op jit(solution)/shard_map/psum | solution.py:56
  482.1 10.7 %fusion.31 = bf16[128,6144]{1,0:T(8,128)(2,1)} fusion(bf16[1,1536,6144]{2,1,0:T(8,128)(2,1)} %param.8, bf16[128,1536]{1,0:T(8,128)(2,1)} %all-reduce.12.cloned.1.call-done, bf16[1,1,128,1536]{3,2,1,0:T(8,128)(2,1)S(1)} %all-gather.7), kind=kOutput, calls=%fused_computation.27 | convolution fusion | flops 2420834304 | bytes 21233664 | tf_op jit(solution)/shard_map/dot_general | solution.py:61
  493.6 34.8 %reduce-scatter.12.cloned.1.call-done = bf16[128,1536]{1,0:T(8,128)(2,1)} async-done(((bf16[128,6144]{1,0:T(8,128)(2,1)}), bf16[128,1536]{1,0:T(8,128)(2,1)}) %reduce-scatter.12.cloned.1.call-update) | async-done | bytes 393232 | tf_op jit(solution)/shard_map/reduce_scatter | solution.py:62
  531.1 2.3 collective-permute-done.3
  534.3 3.1 constant_dynamic-slice_fusion.3
  539.2 35.2 %all-gather.28.cloned.1.call-done = bf16[128,6144]{1,0:T(8,128)(2,1)} async-done(((bf16[128,1536]{1,0:T(8,128)(2,1)}), bf16[128,6144]{1,0:T(8,128)(2,1)}) %all-gather.28.cloned.1.call-update) | async-done | bytes 1572880 | tf_op jit(solution)/shard_map/all_gather | solution.py:50
  574.3 14.0 %fusion.49 = bf16[128,1536]{1,0:T(8,128)(2,1)} fusion(bf16[128,6144]{1,0:T(8,128)(2,1)} %all-gather.28.cloned.1.call-done, bf16[1,1536,6144]{2,1,0:T(8,128)(2,1)} %param.9), kind=kOutput, calls=%fused_computation.33 | convolution fusion | flops 2416115712 | bytes 20840448 | tf_op jit(solution)/shard_map/dot_general | solution.py:53
  589.2 6.7 all-gather.9
  595.9 14.9 %fusion.61 = f32[1536,6144]{1,0:T(8,128)} fusion(bf16[1,128,6144]{2,1,0:T(8,128)(2,1)S(1)} %copy-done.2, bf16[1,1,128,1536]{3,2,1,0:T(8,128)(2,1)S(1)} %all-gather.1), kind=kOutput, calls=%fused_computation.78 | convolution fusion | flops 2417885184 | bytes 39714816 | tf_op jit(solution)/shard_map/dot_general | solution.py:66
  611.7 16.8 %fusion.59 = f32[1536,6144]{1,0:T(8,128)} fusion(bf16[1,1,128,6144]{3,2,1,0:T(8,128)(2,1)} %all-gather.32.cloned.1.call-done, bf16[128,1536]{1,0:T(8,128)(2,1)} %all-reduce.6.cloned.1.call-done, bf16[1,1,128,1536]{3,2,1,0:T(8,128)(2,1)S(1)} %all-gather.1), kind=kOutput, calls=%fused_computation.76 | convolution fusion | flops 2420047872 | bytes 40108032 | tf_op jit(solution)/shard_map/dot_general | solution.py:69
  628.5 14.9 %fusion.121 = f32[1536,6144]{1,0:T(8,128)} fusion(bf16[128,6144]{1,0:T(8,128)(2,1)S(1)} %copy-done.3, bf16[1,1,128,1536]{3,2,1,0:T(8,128)(2,1)S(1)} %copy-done.7), kind=kOutput, calls=%fused_computation.142 | convolution fusion | flops 2417885184 | bytes 39714816 | tf_op jit(solution)/shard_map/dot_general | solution.py:66
  643.4 6.2 all-gather.34.cloned.1.call-done
  649.6 16.7 %fusion.57 = f32[1536,6144]{1,0:T(8,128)} fusion(bf16[1,1,128,6144]{3,2,1,0:T(8,128)(2,1)} %all-gather.34.cloned.1.call-done, bf16[128,1536]{1,0:T(8,128)(2,1)S(1)} %copy-done.20, bf16[1,1,128,1536]{3,2,1,0:T(8,128)(2,1)S(1)} %copy-done.7), kind=kOutput, calls=%fused_computation.74 | convolution fusion | flops 2420047872 | bytes 40108032 | tf_op jit(solution)/shard_map/dot_general | solution.py:69
  666.3 15.4 %fusion.123 = f32[1536,6144]{1,0:T(8,128)} fusion(bf16[128,6144]{1,0:T(8,128)(2,1)S(1)} %copy-done.4, bf16[1,1,128,1536]{3,2,1,0:T(8,128)(2,1)S(1)} %copy-done.9), kind=kOutput, calls=%fused_computation.143 | convolution fusion | flops 2417885184 | bytes 39714816 | tf_op jit(solution)/shard_map/dot_general | solution.py:66
  681.6 5.9 all-gather.36.cloned.1.call-done
  687.5 16.6 %fusion.55 = f32[1536,6144]{1,0:T(8,128)} fusion(bf16[1,1,128,6144]{3,2,1,0:T(8,128)(2,1)} %all-gather.36.cloned.1.call-done, bf16[128,1536]{1,0:T(8,128)(2,1)S(1)} %copy-done.21, bf16[1,1,128,1536]{3,2,1,0:T(8,128)(2,1)S(1)} %copy-done.9), kind=kOutput, calls=%fused_computation.72 | convolution fusion | flops 2420047872 | bytes 40108032 | tf_op jit(solution)/shard_map/dot_general | solution.py:69
  704.1 14.9 %fusion.125 = f32[1536,6144]{1,0:T(8,128)} fusion(bf16[128,6144]{1,0:T(8,128)(2,1)S(1)} %copy-done.5, bf16[1,1,128,1536]{3,2,1,0:T(8,128)(2,1)S(1)} %copy-done.11), kind=kOutput, calls=%fused_computation.144 | convolution fusion | flops 2417885184 | bytes 39714816 | tf_op jit(solution)/shard_map/dot_general | solution.py:66
  719.0 5.9 all-gather.38.cloned.1.call-done
  724.8 16.4 %fusion.53 = f32[1536,6144]{1,0:T(8,128)} fusion(bf16[1,1,128,6144]{3,2,1,0:T(8,128)(2,1)} %all-gather.38.cloned.1.call-done, bf16[128,1536]{1,0:T(8,128)(2,1)S(1)} %copy-done.22, bf16[1,1,128,1536]{3,2,1,0:T(8,128)(2,1)S(1)} %copy-done.11), kind=kOutput, calls=%fused_computation.70 | convolution fusion | flops 2420047872 | bytes 40108032 | tf_op jit(solution)/shard_map/dot_general | solution.py:69
  742.1 25.1 %fusion.1 = bf16[1,1536,6144]{2,1,0:T(8,128)(2,1)} fusion(bf16[128,6144]{1,0:T(8,128)(2,1)S(1)} %copy-done.1, f32[1536,6144]{1,0:T(8,128)} %fusion.125, f32[1536,6144]{1,0:T(8,128)} %fusion.123, f32[1536,6144]{1,0:T(8,128)} %fusion.121, f32[1536,6144]{1,0:T(8,128)} %fusion.61, pred[]{:T(512)S(6)} %and.20, pred[]{:T(512)S(6)} %and.19, pred[]{:T(512)S(6)} %and.18, ...), kind=kOutput, calls=%fused_computation.3 | convolution fusion | flops 2512257024 | bytes 171835392 | tf_op jit(solution)/shard_map/dot_general | solution.py:66
  767.3 10.8 %fusion.34 = bf16[128,6144]{1,0:T(8,128)(2,1)} fusion(bf16[1,1536,6144]{2,1,0:T(8,128)(2,1)} %param.8, bf16[128,1536]{1,0:T(8,128)(2,1)} %all-reduce.14.cloned.1.call-done, bf16[1,1,128,1536]{3,2,1,0:T(8,128)(2,1)S(1)} %copy-done.15), kind=kOutput, calls=%fused_computation.28 | convolution fusion | flops 2420834304 | bytes 21233664 | tf_op jit(solution)/shard_map/dot_general | solution.py:61
  778.1 12.7 %all-gather.40.cloned.1.call-done = bf16[1,1,128,6144]{3,2,1,0:T(8,128)(2,1)} async-done(((bf16[1,1,128,1536]{3,2,1,0:T(8,128)(2,1)}), bf16[1,1,128,6144]{3,2,1,0:T(8,128)(2,1)}) %all-gather.40.cloned.1.call-update) | async-done | bytes 1572880 | tf_op jit(solution)/shard_map/all_gather | solution.py:51
  790.9 25.9 %fusion = bf16[1,1536,6144]{2,1,0:T(8,128)(2,1)} fusion(f32[1536,6144]{1,0:T(8,128)} %fusion.53, f32[1536,6144]{1,0:T(8,128)} %fusion.55, f32[1536,6144]{1,0:T(8,128)} %fusion.57, f32[1536,6144]{1,0:T(8,128)} %fusion.59, pred[]{:T(512)S(6)} %and.20, pred[]{:T(512)S(6)} %and.19, pred[]{:T(512)S(6)} %and.18, pred[]{:T(512)S(6)} %and.17, pred[]{:T(512)S(6)} %and.16, ...), kind=kOutput, calls=%fused_computation.2 | convolution fusion | flops 2514419712 | bytes 172228608 | tf_op jit(solution)/shard_map/dot_general | solution.py:69
  816.8 10.6 %reduce-scatter.14.cloned.1.call-done = bf16[128,1536]{1,0:T(8,128)(2,1)} async-done(((bf16[128,6144]{1,0:T(8,128)(2,1)}), bf16[128,1536]{1,0:T(8,128)(2,1)}) %reduce-scatter.14.cloned.1.call-update) | async-done | bytes 393232 | tf_op jit(solution)/shard_map/reduce_scatter | solution.py:62
  (110 shorter events, 24.9 us)
Async XLA Ops:
  7.2 56.8 %copy-start.16 = (bf16[1,2,64,1536]{3,2,1,0:T(8,128)(2,1)S(1)}, bf16[1,2,64,1536]{3,2,1,0:T(8,128)(2,1)}, u32[]{:S(2)}) copy-start(bf16[1,2,64,1536]{3,2,1,0:T(8,128)(2,1)} %param.7) | copy-start | bytes 1179652
  7.2 42.7 %all-gather.30.cloned.1.call-start = ((), (), s32[]{:S(2)}) async-start(), calls=%async_computation.19 | async-start | bytes 1966080 | tf_op jit(solution)/shard_map/all_gather | solution.py:50
  9.1 80.4 %all-reduce.6.cloned.1.call-start = ((), (), s32[]{:S(2)}) async-start(), calls=%async_computation.5 | async-start | bytes 786432 | tf_op jit(solution)/shard_map/psum | solution.py:56
  63.9 71.9 %copy-start = (bf16[2,128,1536]{2,1,0:T(8,128)(2,1)S(1)}, bf16[2,128,1536]{2,1,0:T(8,128)(2,1)}, u32[]{:S(2)}) copy-start(bf16[2,128,1536]{2,1,0:T(8,128)(2,1)} %param.5) | copy-start | bytes 2359300
  63.9 71.9 %reduce-scatter.6.cloned.1.call-start = ((), (), s32[]{:S(2)}) async-start(), calls=%async_computation.6 | async-start | bytes 1966080 | tf_op jit(solution)/shard_map/reduce_scatter | solution.py:62
  100.2 81.4 %all-gather.22.cloned.1.call-start = ((), (), s32[]{:S(2)}) async-start(), calls=%async_computation.7 | async-start | bytes 1966080 | tf_op jit(solution)/shard_map/all_gather | solution.py:50
  137.0 3.6 collective-permute-start
  141.4 79.0 %all-reduce.8.cloned.1.call-start = ((), (), s32[]{:S(2)}) async-start(), calls=%async_computation.8 | async-start | bytes 786432 | tf_op jit(solution)/shard_map/psum | solution.py:56
  195.5 71.2 %copy-start.12 = (bf16[128,1536]{1,0:T(8,128)(2,1)S(1)}, bf16[128,1536]{1,0:T(8,128)(2,1)}, u32[]{:S(2)}) copy-start(bf16[128,1536]{1,0:T(8,128)(2,1)} %bitcast_select_fusion.6) | copy-start | bytes 1179652
  195.5 71.2 %reduce-scatter.8.cloned.1.call-start = ((), (), s32[]{:S(2)}) async-start(), calls=%async_computation.9 | async-start | bytes 1966080 | tf_op jit(solution)/shard_map/reduce_scatter | solution.py:62
  203.8 122.6 %copy-start.6 = (bf16[1,1,128,1536]{3,2,1,0:T(8,128)(2,1)}, bf16[1,1,128,1536]{3,2,1,0:T(8,128)(2,1)S(1)}, u32[]{:S(2)}) copy-start(bf16[1,1,128,1536]{3,2,1,0:T(8,128)(2,1)S(1)} %all-gather.3) | copy-start | bytes 1179652
  231.1 81.3 %all-gather.24.cloned.1.call-start = ((), (), s32[]{:S(2)}) async-start(), calls=%async_computation.10 | async-start | bytes 1966080 | tf_op jit(solution)/shard_map/all_gather | solution.py:50
  267.9 3.6 collective-permute-start.1
  272.3 79.0 %all-reduce.10.cloned.1.call-start = ((), (), s32[]{:S(2)}) async-start(), calls=%async_computation.11 | async-start | bytes 786432 | tf_op jit(solution)/shard_map/psum | solution.py:56
  326.4 71.2 %copy-start.13 = (bf16[128,1536]{1,0:T(8,128)(2,1)S(1)}, bf16[128,1536]{1,0:T(8,128)(2,1)}, u32[]{:S(2)}) copy-start(bf16[128,1536]{1,0:T(8,128)(2,1)} %bitcast_select_fusion.5) | copy-start | bytes 1179652
  326.4 71.2 %reduce-scatter.10.cloned.1.call-start = ((), (), s32[]{:S(2)}) async-start(), calls=%async_computation.12 | async-start | bytes 1966080 | tf_op jit(solution)/shard_map/reduce_scatter | solution.py:62
  334.7 122.5 %copy-start.8 = (bf16[1,1,128,1536]{3,2,1,0:T(8,128)(2,1)}, bf16[1,1,128,1536]{3,2,1,0:T(8,128)(2,1)S(1)}, u32[]{:S(2)}) copy-start(bf16[1,1,128,1536]{3,2,1,0:T(8,128)(2,1)S(1)} %all-gather.5) | copy-start | bytes 1179652
  362.0 81.3 %all-gather.26.cloned.1.call-start = ((), (), s32[]{:S(2)}) async-start(), calls=%async_computation.13 | async-start | bytes 1966080 | tf_op jit(solution)/shard_map/all_gather | solution.py:50
  398.8 3.6 collective-permute-start.2
  403.2 78.9 %all-reduce.12.cloned.1.call-start = ((), (), s32[]{:S(2)}) async-start(), calls=%async_computation.14 | async-start | bytes 786432 | tf_op jit(solution)/shard_map/psum | solution.py:56
  457.3 71.1 %reduce-scatter.12.cloned.1.call-start = ((), (), s32[]{:S(2)}) async-start(), calls=%async_computation.15 | async-start | bytes 1966080 | tf_op jit(solution)/shard_map/reduce_scatter | solution.py:62
  465.2 16.9 %copy-start.10 = (bf16[1,1,128,1536]{3,2,1,0:T(8,128)(2,1)}, bf16[1,1,128,1536]{3,2,1,0:T(8,128)(2,1)S(1)}, u32[]{:S(2)}) copy-start(bf16[1,1,128,1536]{3,2,1,0:T(8,128)(2,1)S(1)} %all-gather.7) | copy-start | bytes 1179652
  492.7 103.2 %copy-start.2 = (bf16[1,128,6144]{2,1,0:T(8,128)(2,1)S(1)}, bf16[1,128,6144]{2,1,0:T(8,128)(2,1)}, u32[]{:S(2)}) copy-start(bf16[1,128,6144]{2,1,0:T(8,128)(2,1)} %all-gather.30.cloned.1.call-done) | copy-start | bytes 4718596
  492.8 81.5 %all-gather.28.cloned.1.call-start = ((), (), s32[]{:S(2)}) async-start(), calls=%async_computation.16 | async-start | bytes 1966080 | tf_op jit(solution)/shard_map/all_gather | solution.py:50
  529.8 3.6 collective-permute-start.3
  534.2 55.0 %copy-start.19 = (bf16[1,1,64,1536]{3,2,1,0:T(8,128)(2,1)S(1)}, bf16[1,1,64,1536]{3,2,1,0:T(8,128)(2,1)}, u32[]{:S(2)}) copy-start(bf16[1,1,64,1536]{3,2,1,0:T(8,128)(2,1)} %get-tuple-element.16) | copy-start | bytes 589828
  534.2 77.5 %all-gather.32.cloned.1.call-start = ((), (), s32[]{:S(2)}) async-start(), calls=%async_computation.20 | async-start | bytes 1966080 | tf_op jit(solution)/shard_map/all_gather | solution.py:51
  537.4 112.2 %all-gather.34.cloned.1.call-start = ((), (), s32[]{:S(2)}) async-start(), calls=%async_computation.21 | async-start | bytes 1966080 | tf_op jit(solution)/shard_map/all_gather | solution.py:51
  538.0 149.5 %all-gather.36.cloned.1.call-start = ((), (), s32[]{:S(2)}) async-start(), calls=%async_computation.22 | async-start | bytes 1966080 | tf_op jit(solution)/shard_map/all_gather | solution.py:51
  538.5 186.3 %all-gather.38.cloned.1.call-start = ((), (), s32[]{:S(2)}) async-start(), calls=%async_computation.23 | async-start | bytes 1966080 | tf_op jit(solution)/shard_map/all_gather | solution.py:51
  539.1 228.1 %all-reduce.14.cloned.1.call-start = ((), (), s32[]{:S(2)}) async-start(), calls=%async_computation.17 | async-start | bytes 786432 | tf_op jit(solution)/shard_map/psum | solution.py:56
  588.4 202.5 %all-gather.40.cloned.1.call-start = ((), (), s32[]{:S(2)}) async-start(), calls=%async_computation.24 | async-start | bytes 1966080 | tf_op jit(solution)/shard_map/all_gather | solution.py:51
  589.1 238.2 %reduce-scatter.14.cloned.1.call-start = ((), (), s32[]{:S(2)}) async-start(), calls=%async_computation.18 | async-start | bytes 1966080 | tf_op jit(solution)/shard_map/reduce_scatter | solution.py:62
  610.8 17.7 %copy-start.3 = (bf16[128,6144]{1,0:T(8,128)(2,1)S(1)}, bf16[128,6144]{1,0:T(8,128)(2,1)}, u32[]{:S(2)}) copy-start(bf16[128,6144]{1,0:T(8,128)(2,1)} %all-gather.22.cloned.1.call-done) | copy-start | bytes 4718596
  610.8 17.7 %copy-start.7 = (bf16[1,1,128,1536]{3,2,1,0:T(8,128)(2,1)S(1)}, bf16[1,1,128,1536]{3,2,1,0:T(8,128)(2,1)}, u32[]{:S(2)}) copy-start(bf16[1,1,128,1536]{3,2,1,0:T(8,128)(2,1)} %copy-done.6) | copy-start | bytes 1179652
  628.5 21.1 %copy-start.20 = (bf16[128,1536]{1,0:T(8,128)(2,1)S(1)}, bf16[128,1536]{1,0:T(8,128)(2,1)}, u32[]{:S(2)}) copy-start(bf16[128,1536]{1,0:T(8,128)(2,1)} %all-reduce.8.cloned.1.call-done) | copy-start | bytes 1179652
  643.4 22.9 %copy-start.4 = (bf16[128,6144]{1,0:T(8,128)(2,1)S(1)}, bf16[128,6144]{1,0:T(8,128)(2,1)}, u32[]{:S(2)}) copy-start(bf16[128,6144]{1,0:T(8,128)(2,1)} %all-gather.24.cloned.1.call-done) | copy-start | bytes 4718596
  643.4 22.9 %copy-start.9 = (bf16[1,1,128,1536]{3,2,1,0:T(8,128)(2,1)S(1)}, bf16[1,1,128,1536]{3,2,1,0:T(8,128)(2,1)}, u32[]{:S(2)}) copy-start(bf16[1,1,128,1536]{3,2,1,0:T(8,128)(2,1)} %copy-done.8) | copy-start | bytes 1179652
  666.3 21.2 %copy-start.21 = (bf16[128,1536]{1,0:T(8,128)(2,1)S(1)}, bf16[128,1536]{1,0:T(8,128)(2,1)}, u32[]{:S(2)}) copy-start(bf16[128,1536]{1,0:T(8,128)(2,1)} %all-reduce.10.cloned.1.call-done) | copy-start | bytes 1179652
  681.6 22.5 %copy-start.5 = (bf16[128,6144]{1,0:T(8,128)(2,1)S(1)}, bf16[128,6144]{1,0:T(8,128)(2,1)}, u32[]{:S(2)}) copy-start(bf16[128,6144]{1,0:T(8,128)(2,1)} %all-gather.26.cloned.1.call-done) | copy-start | bytes 4718596
  681.6 22.5 %copy-start.11 = (bf16[1,1,128,1536]{3,2,1,0:T(8,128)(2,1)S(1)}, bf16[1,1,128,1536]{3,2,1,0:T(8,128)(2,1)}, u32[]{:S(2)}) copy-start(bf16[1,1,128,1536]{3,2,1,0:T(8,128)(2,1)} %copy-done.10) | copy-start | bytes 1179652
  704.1 20.7 %copy-start.22 = (bf16[128,1536]{1,0:T(8,128)(2,1)S(1)}, bf16[128,1536]{1,0:T(8,128)(2,1)}, u32[]{:S(2)}) copy-start(bf16[128,1536]{1,0:T(8,128)(2,1)} %all-reduce.12.cloned.1.call-done) | copy-start | bytes 1179652
  719.0 23.2 %copy-start.1 = (bf16[128,6144]{1,0:T(8,128)(2,1)S(1)}, bf16[128,6144]{1,0:T(8,128)(2,1)}, u32[]{:S(2)}) copy-start(bf16[128,6144]{1,0:T(8,128)(2,1)} %all-gather.28.cloned.1.call-done) | copy-start | bytes 4718596
  719.0 23.2 %copy-start.15 = (bf16[1,1,128,1536]{3,2,1,0:T(8,128)(2,1)S(1)}, bf16[1,1,128,1536]{3,2,1,0:T(8,128)(2,1)}, u32[]{:S(2)}) copy-start(bf16[1,1,128,1536]{3,2,1,0:T(8,128)(2,1)} %all-gather.9) | copy-start | bytes 1179652
  767.2 23.6 %copy-start.23 = (bf16[128,1536]{1,0:T(8,128)(2,1)S(1)}, bf16[128,1536]{1,0:T(8,128)(2,1)}, u32[]{:S(2)}) copy-start(bf16[128,1536]{1,0:T(8,128)(2,1)} %all-reduce.14.cloned.1.call-done) | copy-start | bytes 1179652
  778.1 49.2 %copy-start.14 = (bf16[128,1536]{1,0:T(8,128)(2,1)S(1)}, bf16[128,1536]{1,0:T(8,128)(2,1)}, u32[]{:S(2)}) copy-start(bf16[128,1536]{1,0:T(8,128)(2,1)} %bitcast_select_fusion.3) | copy-start | bytes 1179652
  778.1 49.2 %copy-start.17 = (bf16[1,2,128,1536]{3,2,1,0:T(8,128)(2,1)S(1)}, bf16[1,2,128,1536]{3,2,1,0:T(8,128)(2,1)}, u32[]{:S(2)}) copy-start(bf16[1,2,128,1536]{3,2,1,0:T(8,128)(2,1)} %copy.17) | copy-start | bytes 2359300
  828.5 0.9 copy-start.18
Sparse Core Ops, SparseCore 0:
  10.1 39.7 all-gather.29
  64.0 25.3 all-reduce.5
  100.3 35.4 reduce-scatter.5
  141.5 39.9 all-gather.21
  195.6 24.7 all-reduce.7
  231.2 35.4 reduce-scatter.7
  272.4 39.9 all-gather.23
  326.5 24.7 all-reduce.9
  362.1 35.4 reduce-scatter.9
  403.3 39.9 all-gather.25
  457.4 24.6 all-reduce.11
  492.9 35.4 reduce-scatter.11
  534.3 39.9 all-gather.27
  575.7 35.8 all-gather.31
  613.6 35.8 all-gather.33
  651.6 35.8 all-gather.35
  688.9 35.8 all-gather.37
  727.0 24.6 all-reduce.13
  753.8 37.0 all-gather.39
  793.0 34.2 reduce-scatter.13
where the time goes:
time: 843 us; the launch traced here: 836 us
  waiting for transfers between devices  456 us (54%)
  matrix products  301 us (36%)
  blocking collectives  40.5 us (5%)
  between operations  14.8 us (2%)
  other arithmetic  9.16 us (1%)
  local copies, waits for them, and re-layouts  8.44 us (1%)
    all_gather x5, waiting for transfers between devices, on_device(): lax.all_gather(current, 'tensor', axis=1, tiled=True)  195 us
    reduce_scatter x5, waiting for transfers between devices, on_device(): lax.psum_scatter(partial_value.astype(jnp.bfloat16), 'tensor', scatter_di...  152 us
    dot_general x5, matrix products, on_device(): lax.dot_general(head_delta, input_cols, contract, preferred_element_type=...  92.4 us
    dot_general x5, matrix products, on_device(): lax.dot_general(activated, grad_cols, contract, preferred_element_type=jn...  85.1 us
    dot_general x5, matrix products, on_device(): lax.dot_general(grad_cols, local_out, (((1,), (1,)), ((), ())), preferred...  69.8 us
    psum x5, waiting for transfers between devices, on_device(): lax.psum(head_part.astype(jnp.bfloat16), 'dp').astype(jnp.float32)  65.3 us
    dot_general x5, matrix products, on_device(): jnp.dot(head_delta, local_in, preferred_element_type=jnp.float32)  53.6 us
    all_gather x5, blocking collectives, on_device(): pre_all = lax.all_gather(pre_local, 'dp', axis=0, tiled=True)  40.5 us
  transfers between devices with their start and end apart: 24, of which 23 were waited for; matrix products, arithmetic and copies ran while one was open for 25% of the time, Pallas kernels for 0%

commit v1 on v0

--- a/solution.py
+++ b/solution.py
@@ -1,8 +1,11 @@
+import functools
 import math
 
 import jax
 import jax.numpy as jnp
 from jax import lax
+from jax.experimental import pallas as pl
+from jax.experimental.pallas import tpu as pltpu
 from jax.sharding import PartitionSpec as P
 
 
@@ -23,7 +26,7 @@
     return (activ, slope)
 
 
-def on_device(grad_top, inputs, pre, weight_in, weight_out):
+def general_device(grad_top, inputs, pre, weight_in, weight_out):
     sections = lax.axis_size("pipe")
     section = lax.axis_index("pipe")
     micro = grad_top.shape[0]
@@ -83,6 +86,366 @@
     )
 
 
+MESH = pl.DeviceIdType.MESH
+CHUNK = 64
+HEAD_TILE = 256
+COL_TILE = 512
+VMEM_BYTES = 62 * 2**20
+
+
+def chain_kernel(
+    dims,
+    gtop, pre, inputs, win, wout,
+    gall_o, xall_o, hd_o, act_o, sg_o,
+    wi, wo, gbuf, rs_out, rs_in, dp_out, dp_in, slope, hg, pre_s, act, hd, newg, xs,
+    w_sem, top_send, top_own, g_send, g_recv, rs_send, rs_recv, dp_send, dp_recv,
+    pre_send, pre_recv, pre_own, x_send, x_recv, x_own, out_sem,
+):
+    sections, dps, tensors, chunks, chunk_rows, micro, block_rows = dims
+    s = lax.axis_index("pipe")
+    d = lax.axis_index("dp")
+    t = lax.axis_index("tensor")
+    heads, wide = wo.shape
+    cols = wide // tensors
+    is_top = s == sections - 1
+    has_next = s > 0
+
+    def wrap(value, size):
+        return lax.rem(value + size, size)
+
+    def column(index):
+        return pl.ds(pl.multiple_of(index * cols, 128), cols)
+
+    def row(c):
+        return pl.ds(pl.multiple_of(c * chunk_rows, chunk_rows), chunk_rows)
+
+    def remote(src, dst, send, recv, device):
+        return pltpu.make_async_remote_copy(
+            src_ref=src, dst_ref=dst, send_sem=send, recv_sem=recv,
+            device_id=device, device_id_type=MESH,
+        )
+
+    copy_wo = pltpu.make_async_copy(wout, wo, w_sem.at[0])
+    copy_wi = pltpu.make_async_copy(win, wi, w_sem.at[1])
+
+    barrier = pltpu.get_barrier_semaphore()
+    for k in range(1, tensors):
+        pl.semaphore_signal(
+            barrier, inc=1, device_id=(s, d, wrap(t + k, tensors)), device_id_type=MESH)
+    for k in range(1, dps):
+        pl.semaphore_signal(
+            barrier, inc=1, device_id=(s, wrap(d + k, dps), t), device_id_type=MESH)
+
+    for hop in (1, sections - 1):
+        for k in range(tensors):
+            pl.semaphore_signal(
+                barrier, inc=1, device_id=(wrap(s + hop, sections), d, k), device_id_type=MESH)
+    pl.semaphore_wait(barrier, (tensors - 1) + (dps - 1) + 2 * tensors)
+
+    def top_copy(c, k):
+        return remote(
+            gtop.at[row(c), :], gbuf.at[row(c), column(t)],
+            top_send.at[c, k - 1], g_recv.at[c, t], (s, d, wrap(t + k, tensors)))
+
+    def top_local(c):
+        return pltpu.make_async_copy(
+            gtop.at[row(c), :], gbuf.at[row(c), column(t)], top_own.at[c])
+
+    def relay_copy(c, k):
+        return remote(
+            newg.at[row(c), :], gbuf.at[row(c), column(t)],
+            g_send.at[c, k], g_recv.at[c, t], (s - 1, d, k))
+
+    def arrival(c, source):
+        return remote(
+            newg.at[row(c), :], gbuf.at[row(c), column(source)],
+            g_send.at[c, 0], g_recv.at[c, source], (s, d, t))
+
+    def pre_copy(m, k):
+        return remote(
+            pre.at[m], pre_s.at[pl.ds(pl.multiple_of((m * dps + d) * block_rows, 16), block_rows), :],
+            pre_send.at[m, k - 1], pre_recv.at[m, k - 1], (s, wrap(d + k, dps), t))
+
+    def pre_arrival(m, k):
+        source = wrap(d - k, dps)
+        return remote(
+            pre.at[m], pre_s.at[pl.ds(pl.multiple_of((m * dps + source) * block_rows, 16), block_rows), :],
+            pre_send.at[m, k - 1], pre_recv.at[m, k - 1], (s, wrap(d + k, dps), t))
+
+    def pre_local(m):
+        return pltpu.make_async_copy(
+            pre.at[m], pre_s.at[pl.ds(pl.multiple_of((m * dps + d) * block_rows, 16), block_rows), :],
+            pre_own.at[m])
+
+    def x_copy(k):
+        return remote(
+            inputs, xall_o.at[:, column(t)],
+            x_send.at[k - 1], x_recv.at[k - 1], (s, d, wrap(t + k, tensors)))
+
+    def x_arrival(k):
+        return remote(
+            inputs, xall_o.at[:, column(wrap(t - k, tensors))],
+            x_send.at[k - 1], x_recv.at[k - 1], (s, d, wrap(t + k, tensors)))
+
+    def dp_copy(c, k):
+        return remote(
+            dp_out.at[row(c), :], dp_in.at[k - 1, row(c), :],
+            dp_send.at[c, k - 1], dp_recv.at[c, k - 1], (s, wrap(d + k, dps), t))
+
+    def rs_copy(c, k):
+        target = wrap(t + k, tensors)
+        return remote(
+            rs_out.at[row(c), column(target)], rs_in.at[k - 1, row(c), :],
+            rs_send.at[c, k - 1], rs_recv.at[c, k - 1], (s, d, target))
+
+    for m in range(micro):
+        for k in range(1, dps):
+            pre_copy(m, k).start()
+        pre_local(m).start()
+
+    @pl.when(is_top)
+    def _():
+        @pl.loop(0, chunks)
+        def _(c):
+            top_local(c).start()
+            for k in range(1, tensors):
+                top_copy(c, k).start()
+
+    copy_wo.start()
+    copy_wi.start()
+    early = 2 * s < sections
+
+    @pl.when(early)
+    def _():
+        for k in range(1, tensors):
+            x_copy(k).start()
+
+    x_in = pltpu.make_async_copy(inputs, xs, x_own.at[0])
+    x_out = pltpu.make_async_copy(xs, xall_o.at[:, column(t)], x_own.at[1])
+    x_in.start()
+
+    for m in range(micro):
+        pre_local(m).wait()
+        for k in range(1, dps):
+            pre_arrival(m, k).wait_recv()
+
+    @pl.loop(0, pre_s.shape[0] // 16)
+    def _(b):
+        rows = pl.ds(pl.multiple_of(b * 16, 16), 16)
+        activ, steep = gelu_pair(pre_s[rows, :].astype(jnp.float32))
+        act[rows, :] = activ.astype(jnp.bfloat16)
+        slope[rows, :] = steep
+
+    x_in.wait()
+    x_out.start()
+    act_out = pltpu.make_async_copy(act, act_o, out_sem.at[0])
+    act_out.start()
+    copy_wo.wait()
+
+    def chunk_step(c):
+        @pl.when(is_top)
+        def _():
+            top_local(c).wait()
+            for k in range(1, tensors):
+                arrival(c, wrap(t + k, tensors)).wait_recv()
+
+        @pl.when(jnp.logical_not(is_top))
+        def _():
+            for k in range(tensors):
+                arrival(c, k).wait_recv()
+
+        @pl.loop(0, heads // HEAD_TILE)
+        def _(j):
+            tile = pl.ds(pl.multiple_of(j * HEAD_TILE, HEAD_TILE), HEAD_TILE)
+            part = lax.dot_general(
+                gbuf[row(c), :], wo[tile, :], (((1,), (1,)), ((), ())),
+                preferred_element_type=jnp.float32)
+            hg[:, tile] = part
+            dp_out[row(c), tile] = part.astype(jnp.bfloat16)
+
+        for k in range(1, dps):
+            dp_copy(c, k).start()
+
+        @pl.when(c == 0)
+        def _():
+            copy_wi.wait()
+
+        for k in range(1, dps):
+            dp_copy(c, k).wait_recv()
+        total = hg[...]
+        for k in range(1, dps):
+            total = total + dp_in[k - 1, row(c), :].astype(jnp.float32)
+        hd[row(c), :] = (total * slope[row(c), :]).astype(jnp.bfloat16)
+
+        for k in list(range(1, tensors)) + [0]:
+            base = wrap(t + k, tensors) * cols
+
+            @pl.loop(0, cols // COL_TILE)
+            def _(j):
+                tile = pl.ds(pl.multiple_of(base + j * COL_TILE, 128), COL_TILE)
+                rs_out[row(c), tile] = jnp.dot(
+                    hd[row(c), :], wi[:, tile], preferred_element_type=jnp.float32
+                ).astype(jnp.bfloat16)
+
+            if k:
+                rs_copy(c, k).start()
+
+        for k in range(1, tensors):
+            rs_copy(c, k).wait_recv()
+        summed = rs_out[row(c), column(t)].astype(jnp.float32)
+        for k in range(1, tensors):
+            summed = summed + rs_in[k - 1, row(c), :].astype(jnp.float32)
+        newg[row(c), :] = (
+            gbuf[row(c), column(t)].astype(jnp.float32) + summed).astype(jnp.bfloat16)
+
+        @pl.when(has_next)
+        def _():
+            for k in range(tensors):
+                relay_copy(c, k).start()
+
+    @pl.loop(0, chunks)
+    def _(c):
+        chunk_step(c)
+
+    @pl.when(jnp.logical_not(early))
+    def _():
+        for k in range(1, tensors):
+            x_copy(k).start()
+
+    outs = [
+        pltpu.make_async_copy(gbuf, gall_o, out_sem.at[1]),
+        pltpu.make_async_copy(hd, hd_o, out_sem.at[2]),
+        pltpu.make_async_copy(newg, sg_o, out_sem.at[3]),
+    ]
+    for copy in outs:
+        copy.start()
+
+    for m in range(micro):
+        for k in range(1, dps):
+            pre_copy(m, k).wait_send()
+
+    @pl.loop(0, chunks)
+    def _(c):
+        for k in range(1, dps):
+            dp_copy(c, k).wait_send()
+        for k in range(1, tensors):
+            rs_copy(c, k).wait_send()
+
+        @pl.when(is_top)
+        def _():
+            for k in range(1, tensors):
+                top_copy(c, k).wait_send()
+
+        @pl.when(has_next)
+        def _():
+            for k in range(tensors):
+                relay_copy(c, k).wait_send()
+
+    x_out.wait()
+    act_out.wait()
+    for copy in outs:
+        copy.wait()
+    for k in range(1, tensors):
+        x_copy(k).wait_send()
+        x_arrival(k).wait_recv()
+
+
+def chain(sizes, gtop, pre, inputs, win, wout):
+    sections, dps, tensors = sizes
+    rows, cols = gtop.shape
+    micro, block_rows, heads = pre.shape
+    wide = wout.shape[1]
+    chunks = rows // CHUNK
+    dims = (sections, dps, tensors, chunks, CHUNK, micro, block_rows)
+    bf16, f32 = jnp.bfloat16, jnp.float32
+    anywhere = pl.BlockSpec(memory_space=pl.ANY)
+    dma = pltpu.SemaphoreType.DMA
+    return pl.pallas_call(
+        functools.partial(chain_kernel, dims),
+        out_shape=(
+            jax.ShapeDtypeStruct((rows, wide), bf16),
+            jax.ShapeDtypeStruct((rows, wide), bf16),
+            jax.ShapeDtypeStruct((rows, heads), bf16),
+            jax.ShapeDtypeStruct((rows, heads), bf16),
+            jax.ShapeDtypeStruct((rows, cols), bf16),
+        ),
+        in_specs=[anywhere] * 5,
+        out_specs=(anywhere,) * 5,
+        scratch_shapes=[
+            pltpu.VMEM((heads, wide), bf16),
+            pltpu.VMEM((heads, wide), bf16),
+            pltpu.VMEM((rows, wide), bf16),
+            pltpu.VMEM((rows, wide), bf16),
+            pltpu.VMEM((tensors - 1, rows, cols), bf16),
+            pltpu.VMEM((rows, heads), bf16),
+            pltpu.VMEM((dps - 1, rows, heads), bf16),
+            pltpu.VMEM((rows, heads), f32),
+            pltpu.VMEM((CHUNK, heads), f32),
+            pltpu.VMEM((rows, heads), bf16),
+            pltpu.VMEM((rows, heads), bf16),
+            pltpu.VMEM((rows, heads), bf16),
+            pltpu.VMEM((rows, cols), bf16),
+            pltpu.VMEM((rows, cols), bf16),
+            dma((2,)),
+            dma((chunks, tensors - 1)),
+            dma((chunks,)),
+            dma((chunks, tensors)),
+            dma((chunks, tensors)),
+            dma((chunks, tensors - 1)),
+            dma((chunks, tensors - 1)),
+            dma((chunks, dps - 1)),
+            dma((chunks, dps - 1)),
+            dma((micro, dps - 1)),
+            dma((micro, dps - 1)),
+            dma((micro,)),
+            dma((tensors - 1,)),
+            dma((tensors - 1,)),
+            dma((2,)),
+            dma((4,)),
+        ],
+        compiler_params=pltpu.CompilerParams(
+            collective_id=0, has_side_effects=True, vmem_limit_bytes=VMEM_BYTES),
+        name="chain",
+    )(gtop, pre, inputs, win, wout)
+
+
+def kernel_fits(sizes, grad_top, pre, weight_out):
+    sections, dps, tensors = sizes
+    micro, tokens, cols = grad_top.shape
+    heads, wide = weight_out.shape[1:]
+    rows = micro * tokens
+    need = 4 * heads * wide + 2 * rows * (3 * wide + (7 + dps) * heads + 2 * cols)
+    return (
+        dps > 1 and tensors > 1 and sections > 1
+        and cols % COL_TILE == 0 and heads % HEAD_TILE == 0
+        and rows % CHUNK == 0 and pre.shape[2] % 16 == 0
+        and need + 4 * CHUNK * heads < VMEM_BYTES - 2**21
+    )
+
+
+def on_device(grad_top, inputs, pre, weight_in, weight_out):
+    sizes = tuple(lax.axis_size(name) for name in ("pipe", "dp", "tensor"))
+    if not kernel_fits(sizes, grad_top, pre, weight_out):
+        return general_device(grad_top, inputs, pre, weight_in, weight_out)
+    cols = grad_top.shape[-1]
+    gall, xall, head_delta, activated, new_grad = chain(
+        sizes,
+        grad_top.reshape(-1, cols),
+        pre[0],
+        inputs[0].reshape(-1, cols),
+        weight_in[0],
+        weight_out[0],
+    )
+    contract = (((0,), (0,)), ((), ()))
+    grad_out = lax.dot_general(activated, gall, contract, preferred_element_type=jnp.float32)
+    grad_in = lax.dot_general(head_delta, xall, contract, preferred_element_type=jnp.float32)
+    return (
+        grad_in.astype(jnp.bfloat16)[None],
+        grad_out.astype(jnp.bfloat16)[None],
+        new_grad.reshape(grad_top.shape)[None],
+    )
+
+
 def solution(mesh):
     placed = (
         P(None, None, ("dp", "tensor")),

time: 843 us -> 311 us (0.37)
  waiting for transfers between devices: 456 us -> 0 us
  Pallas kernels: 0 us -> 289 us
  matrix products: 301 us -> 20.8 us
  blocking collectives: 40.5 us -> 0 us
  between operations: 14.8 us -> 0.67 us
  other arithmetic: 9.16 us -> 0 us
    pallas_call x0 -> x1, Pallas kernels: none -> 289 us  [chain(): pl.pallas_call(functools.partial(chain_kernel, dims), out_shape=(jax.Shap...]
    dot_general x20 -> x2, matrix products: 301 us -> 20.8 us  [the longest x1 11.3 us: on_device(): lax.dot_general(head_delta, xall, contract, preferred_element_type=jnp.fl...]
    all_gather x10 -> x0, waiting for transfers between devices: 227 us -> none  [the longest x5 195 us: on_device(): lax.all_gather(current, 'tensor', axis=1, tiled=True)]
    reduce_scatter x5 -> x0, waiting for transfers between devices: 152 us -> none  [on_device(): lax.psum_scatter(partial_value.astype(jnp.bfloat16), 'tensor', scatter_di...]
    psum x5 -> x0, waiting for transfers between devices: 65.3 us -> none  [on_device(): lax.psum(head_part.astype(jnp.bfloat16), 'dp').astype(jnp.float32)]
    all_gather x5 -> x0, blocking collectives: 40.5 us -> none  [on_device(): pre_all = lax.all_gather(pre_local, 'dp', axis=0, tiled=True)]
    ppermute x4 -> x0, waiting for transfers between devices: 9.26 us -> none  [shifted(): return lax.ppermute(block, axis, route)]
  transfers between devices with their start and end apart: 24 -> 0, of which waited for: 23 -> 0; matrix products, arithmetic and copies ran while one was open for 25% -> 0% of each run, Pallas kernels for 0% -> 0%
where the time goes in v1:
time: 311 us
  Pallas kernels  289 us (93%)
  matrix products  20.8 us (7%)
    pallas_call x1, Pallas kernels, chain(): pl.pallas_call(functools.partial(chain_kernel, dims), out_shape=(jax.Shap...  289 us
    dot_general x1, matrix products, on_device(): lax.dot_general(head_delta, xall, contract, preferred_element_type=jnp.fl...  11.3 us
    dot_general x1, matrix products, on_device(): lax.dot_general(activated, gall, contract, preferred_element_type=jnp.flo...  9.51 us

profile of v1, /device:TPU:0, one launch (start us, length us, event | category | flops | bytes accessed | tf_op | source)
XLA Modules:
  0.0 311.2 jit_solution(1550578768641652900)
XLA Ops:
  0.6 288.8 %chain.1 = (bf16[256,6144]{1,0:T(8,128)(2,1)}, bf16[256,6144]{1,0:T(8,128)(2,1)}, bf16[256,1536]{1,0:T(8,128)(2,1)}, bf16[256,1536]{1,0:T(8,128)(2,1)}, bf16[256,1536]{1,0:T(8,128)(2,1)}) custom-call(bf16[256,1536]{1,0:T(8,128)(2,1)} %bitcast.17, bf16[2,64,1536]{2,1,0:T(8,128)(2,1)} %bitcast.19, bf16[256,1536]{1,0:T(8,128)(2,1)} %bitcast.18, ...), custom_call_target="tpu_custom_call" | custom-call | tf_op jit(solution)/shard_map/chain/pallas_call | solution.py:363
  289.5 0.0 copy-start
  289.5 0.0 copy-start.1
  289.5 0.0 copy-start.2
  289.5 11.3 %fusion = bf16[1,1536,6144]{2,1,0:T(8,128)(2,1)} fusion(bf16[256,1536]{1,0:T(8,128)(2,1)} %get-tuple-element.8, bf16[256,6144]{1,0:T(8,128)(2,1)} %get-tuple-element.9), kind=kOutput, calls=%fused_computation.2 | convolution fusion | flops 4841275392 | bytes 22806528 | tf_op jit(solution)/shard_map/dot_general | solution.py:441
  300.8 0.0 copy-done
  300.8 0.0 copy-done.1
  300.8 9.5 %fusion.1 = bf16[1,1536,6144]{2,1,0:T(8,128)(2,1)} fusion(bf16[256,1536]{1,0:T(8,128)(2,1)S(1)} %copy-done.1, bf16[256,6144]{1,0:T(8,128)(2,1)S(1)} %copy-done), kind=kOutput, calls=%fused_computation.3 | convolution fusion | flops 4841275392 | bytes 22806528 | tf_op jit(solution)/shard_map/dot_general | solution.py:440
  310.3 0.0 copy-done.2
  310.3 0.9 copy.9
Async XLA Ops:
  289.5 11.3 %copy-start = (bf16[256,6144]{1,0:T(8,128)(2,1)S(1)}, bf16[256,6144]{1,0:T(8,128)(2,1)}, u32[]{:S(2)}) copy-start(bf16[256,6144]{1,0:T(8,128)(2,1)} %get-tuple-element.11) | copy-start | bytes 9437188
  289.5 11.3 %copy-start.1 = (bf16[256,1536]{1,0:T(8,128)(2,1)S(1)}, bf16[256,1536]{1,0:T(8,128)(2,1)}, u32[]{:S(2)}) copy-start(bf16[256,1536]{1,0:T(8,128)(2,1)} %get-tuple-element.10) | copy-start | bytes 2359300
  289.5 20.8 %copy-start.2 = (bf16[256,1536]{1,0:T(8,128)(2,1)S(1)}, bf16[256,1536]{1,0:T(8,128)(2,1)}, u32[]{:S(2)}) copy-start(bf16[256,1536]{1,0:T(8,128)(2,1)} %get-tuple-element.12) | copy-start | bytes 2359300

commit v2 on v1

--- a/solution.py
+++ b/solution.py
@@ -88,7 +88,7 @@
 
 MESH = pl.DeviceIdType.MESH
 CHUNK = 64
-HEAD_TILE = 256
+HEAD_TILE = 512
 COL_TILE = 512
 VMEM_BYTES = 62 * 2**20
 
@@ -242,7 +242,7 @@
     act_out.start()
     copy_wo.wait()
 
-    def chunk_step(c):
+    def head_step(c):
         @pl.when(is_top)
         def _():
             top_local(c).wait()
@@ -266,6 +266,7 @@
         for k in range(1, dps):
             dp_copy(c, k).start()
 
+    def delta_step(c):
         @pl.when(c == 0)
         def _():
             copy_wi.wait()
@@ -278,18 +279,14 @@
         hd[row(c), :] = (total * slope[row(c), :]).astype(jnp.bfloat16)
 
         for k in list(range(1, tensors)) + [0]:
-            base = wrap(t + k, tensors) * cols
-
-            @pl.loop(0, cols // COL_TILE)
-            def _(j):
-                tile = pl.ds(pl.multiple_of(base + j * COL_TILE, 128), COL_TILE)
-                rs_out[row(c), tile] = jnp.dot(
-                    hd[row(c), :], wi[:, tile], preferred_element_type=jnp.float32
-                ).astype(jnp.bfloat16)
-
+            target = column(wrap(t + k, tensors))
+            rs_out[row(c), target] = jnp.dot(
+                hd[row(c), :], wi[:, target], preferred_element_type=jnp.float32
+            ).astype(jnp.bfloat16)
             if k:
                 rs_copy(c, k).start()
 
+    def sum_step(c):
         for k in range(1, tensors):
             rs_copy(c, k).wait_recv()
         summed = rs_out[row(c), column(t)].astype(jnp.float32)
@@ -303,9 +300,13 @@
             for k in range(tensors):
                 relay_copy(c, k).start()
 
+    head_step(0)
+
     @pl.loop(0, chunks)
     def _(c):
-        chunk_step(c)
+        delta_step(c)
+        pl.when(c + 1 < chunks)(lambda: head_step(c + 1))
+        sum_step(c)
 
     @pl.when(jnp.logical_not(early))
     def _():

time: 311 us -> 302 us (0.971)
  Pallas kernels: 289 us -> 279 us
    pallas_call x1, Pallas kernels: 289 us -> 279 us  [chain(): pl.pallas_call(functools.partial(chain_kernel, dims), out_shape=(jax.Shap...]
where the time goes in v2:
time: 302 us; the launch traced here: 301 us
  Pallas kernels  279 us (92%)
  matrix products  20.8 us (7%)
    pallas_call x1, Pallas kernels, chain(): pl.pallas_call(functools.partial(chain_kernel, dims), out_shape=(jax.Shap...  279 us
    dot_general x1, matrix products, on_device(): lax.dot_general(head_delta, xall, contract, preferred_element_type=jnp.fl...  11.3 us
    dot_general x1, matrix products, on_device(): lax.dot_general(activated, gall, contract, preferred_element_type=jnp.flo...  9.51 us

profile of v2, /device:TPU:0, one launch (start us, length us, event | category | flops | bytes accessed | tf_op | source)
XLA Modules:
  0.0 301.4 jit_solution(9381843849318286976)
XLA Ops:
  0.6 279.1 %chain.1 = (bf16[256,6144]{1,0:T(8,128)(2,1)}, bf16[256,6144]{1,0:T(8,128)(2,1)}, bf16[256,1536]{1,0:T(8,128)(2,1)}, bf16[256,1536]{1,0:T(8,128)(2,1)}, bf16[256,1536]{1,0:T(8,128)(2,1)}) custom-call(bf16[256,1536]{1,0:T(8,128)(2,1)} %bitcast.17, bf16[2,64,1536]{2,1,0:T(8,128)(2,1)} %bitcast.19, bf16[256,1536]{1,0:T(8,128)(2,1)} %bitcast.18, ...), custom_call_target="tpu_custom_call" | custom-call | tf_op jit(solution)/shard_map/chain/pallas_call | solution.py:364
  279.7 0.0 copy-start
  279.7 0.0 copy-start.1
  279.7 0.0 copy-start.2
  279.7 11.3 %fusion = bf16[1,1536,6144]{2,1,0:T(8,128)(2,1)} fusion(bf16[256,1536]{1,0:T(8,128)(2,1)} %get-tuple-element.8, bf16[256,6144]{1,0:T(8,128)(2,1)} %get-tuple-element.9), kind=kOutput, calls=%fused_computation.2 | convolution fusion | flops 4841275392 | bytes 22806528 | tf_op jit(solution)/shard_map/dot_general | solution.py:442
  291.0 0.0 copy-done
  291.0 0.0 copy-done.1
  291.0 9.5 %fusion.1 = bf16[1,1536,6144]{2,1,0:T(8,128)(2,1)} fusion(bf16[256,1536]{1,0:T(8,128)(2,1)S(1)} %copy-done.1, bf16[256,6144]{1,0:T(8,128)(2,1)S(1)} %copy-done), kind=kOutput, calls=%fused_computation.3 | convolution fusion | flops 4841275392 | bytes 22806528 | tf_op jit(solution)/shard_map/dot_general | solution.py:441
  300.5 0.0 copy-done.2
  300.5 0.9 copy.9
Async XLA Ops:
  279.7 11.3 %copy-start = (bf16[256,6144]{1,0:T(8,128)(2,1)S(1)}, bf16[256,6144]{1,0:T(8,128)(2,1)}, u32[]{:S(2)}) copy-start(bf16[256,6144]{1,0:T(8,128)(2,1)} %get-tuple-element.11) | copy-start | bytes 9437188
  279.7 11.3 %copy-start.1 = (bf16[256,1536]{1,0:T(8,128)(2,1)S(1)}, bf16[256,1536]{1,0:T(8,128)(2,1)}, u32[]{:S(2)}) copy-start(bf16[256,1536]{1,0:T(8,128)(2,1)} %get-tuple-element.10) | copy-start | bytes 2359300
  279.7 20.8 %copy-start.2 = (bf16[256,1536]{1,0:T(8,128)(2,1)S(1)}, bf16[256,1536]{1,0:T(8,128)(2,1)}, u32[]{:S(2)}) copy-start(bf16[256,1536]{1,0:T(8,128)(2,1)} %get-tuple-element.12) | copy-start | bytes 2359300
